TPU v7x, 512 devices: a whole 4x4x16 slice. The times are simulated.
512 devices in a mesh: section: 16 (over z), batch: 32 (over x, y, core).
Axes of the slice: x: 4, y: 4, z: 16, core: 2. Of those that a mesh axis runs over, the one named last changes fastest.
Arguments:
- images: bfloat16 [32, 256, 1536], P('batch'), may hold values from -10 to 10
- weights: bfloat16 [16, 6, 256, 256], P('section'), may hold values from -0.375 to 0.375
- bn_mean: float32 [16, 1536], P('section'), may hold values from -3 to 3
- bn_var: float32 [16, 1536], P('section'), may hold values from 0.25 to 2
- bn_gain: float32 [16, 1536], P('section'), may hold values from 0.1 to 1.9
- bn_bias: float32 [16, 1536], P('section'), may hold values from -3 to 3
Outputs:
- image_grad: bfloat16 [32, 256, 1536], P('batch', 'section')
- loss_value: float32 [], replicated
All inputs are finite; a program needn't handle non-finite values.
Results may differ from a plain program's by a relative error of at most 0.013.
Values may be sent and summed in bfloat16 or wider, within the bound.
No kernel may reach another device: no remote copies, remote signals or barrier semaphores. Data moves between devices by JAX's collectives and lax.ppermute only.
A program may use at most 64 MiB of HBM per device.

v0:
```python
import jax
import jax.numpy as jnp
from jax import lax
from jax.sharding import PartitionSpec as P

BLOCK = 512
MICRO = 8
EPS = 1e-05
HIGHEST = lax.Precision.HIGHEST


def from_behind(value, axis, steps):
    count = lax.axis_size(axis)
    first, last = (max(0, -steps), min(count, count - steps))
    return lax.ppermute(value, axis, [(source, source + steps) for source in range(first, last)])


def group_forward(hidden, weight):
    row_total = hidden.shape[0]
    groups, in_width, out_width = weight.shape
    pieces = hidden.reshape(row_total, groups, in_width)
    result = jnp.einsum("rgi,gio->rgo", pieces, weight, preferred_element_type=jnp.float32)
    return result.reshape(row_total, groups * out_width)


def group_backward(upstream, weight):
    row_total = upstream.shape[0]
    groups, in_width, out_width = weight.shape
    pieces = upstream.reshape(row_total, groups, out_width)
    result = jnp.einsum("rgo,gio->rgi", pieces, weight, preferred_element_type=jnp.float32)
    return result.reshape(row_total, groups * in_width)


def block_gram(pre_act, center, block_width):
    row_total, channels = pre_act.shape
    centered = (pre_act - center).reshape(row_total, channels // block_width, block_width)
    return jnp.einsum("rbi,rbj->bij", centered, centered, precision=HIGHEST)


def shards(images, weights, bn_mean, bn_var, bn_gain, bn_bias):
    sections = lax.axis_size("section")
    position = lax.axis_index("section")
    group_rows = images.shape[1]
    channels = images.shape[2]
    micro_rows = group_rows // MICRO
    block_count = channels // BLOCK
    row_total = group_rows * lax.axis_size("batch")
    weight = weights[0]
    run_mean = bn_mean[0]
    run_var = bn_var[0]
    bn_scale = bn_gain[0] * lax.rsqrt(run_var + EPS)
    bn_shift = bn_bias[0]
    source = images[0].reshape(MICRO, micro_rows, channels)
    tick_count = MICRO + sections - 1
    gram_shape = (1, 1, 1)
    stored_type = jnp.float32

    def forward_tick(tick_index, loop_vars):
        incoming, stored, sum_pre, sum_gram = loop_vars
        offset_raw = tick_index - position
        in_range = (offset_raw >= 0) & (offset_raw < MICRO)
        slot_index = jnp.clip(offset_raw, 0, MICRO - 1)
        entering = lax.dynamic_index_in_dim(source, slot_index, 0, keepdims=False)
        hidden = jnp.where(position == 0, entering, incoming)

        def forward_active_step(hidden_in):
            pre_act = group_forward(hidden_in, weight)
            emitted = jax.nn.silu((pre_act - run_mean) * bn_scale + bn_shift).astype(jnp.bfloat16)
            block_sums = jnp.zeros(gram_shape, jnp.float32)
            return (pre_act, emitted, jnp.sum(pre_act, axis=0), block_sums)

        def forward_bubble_step(hidden_in):
            return (
                jnp.zeros((micro_rows, channels), jnp.float32),
                jnp.zeros((micro_rows, channels), jnp.bfloat16),
                jnp.zeros((channels,), jnp.float32),
                jnp.zeros(gram_shape, jnp.float32),
            )

        pre_act, emitted, part_sum, block_sums = lax.cond(
            in_range, forward_active_step, forward_bubble_step, hidden
        )
        previous = lax.dynamic_index_in_dim(stored, slot_index, 0, keepdims=False)
        stored = lax.dynamic_update_index_in_dim(
            stored, jnp.where(in_range, pre_act, previous), slot_index, 0
        )
        incoming = from_behind(emitted, "section", 1)
        return (incoming, stored, sum_pre + part_sum, sum_gram + block_sums)

    start_vars = (
        jnp.zeros((micro_rows, channels), jnp.bfloat16),
        jnp.zeros((MICRO, micro_rows, channels), stored_type),
        jnp.zeros((channels,), jnp.float32),
        jnp.zeros(gram_shape, jnp.float32),
    )
    incoming, stored, sum_pre, sum_gram = lax.fori_loop(0, tick_count, forward_tick, start_vars)
    total_sum = lax.psum(sum_pre, "batch")
    batch_mean = total_sum / row_total
    flat_saved = stored.reshape(group_rows, channels)
    covariance = lax.psum(block_gram(flat_saved, batch_mean, BLOCK), "batch") / row_total
    var_blocks = run_var.reshape(block_count, BLOCK)
    deviation = covariance - var_blocks[:, :, None] * jnp.eye(BLOCK, dtype=jnp.float32)[None]
    layer_term = jnp.sum((batch_mean - run_mean) ** 2) + 0.25 * jnp.sum(deviation**2)
    loss_value = lax.psum(layer_term, "section") / (sections * channels)
    mean_pull = 2.0 * (batch_mean - run_mean)

    def backward_tick(tick_index, loop_vars):
        incoming, image_grads = loop_vars
        offset_raw = tick_index - (sections - 1 - position)
        in_range = (offset_raw >= 0) & (offset_raw < MICRO)
        slot_index = jnp.clip(offset_raw, 0, MICRO - 1)
        stored_item = lax.dynamic_index_in_dim(stored, slot_index, 0, keepdims=False)

        def backward_active_step(operands):
            item_in, upstream = operands
            active = (item_in - run_mean) * bn_scale + bn_shift
            sig_value = jax.nn.sigmoid(active)
            silu_slope = sig_value * (1.0 + active * (1.0 - sig_value))
            centered = (item_in - batch_mean).reshape(micro_rows, block_count, BLOCK)
            cov_pull = jnp.einsum("rbi,bij->rbj", centered, deviation, precision=HIGHEST).reshape(
                micro_rows, channels
            )
            pre_grad = (
                upstream.astype(jnp.float32) * silu_slope * bn_scale + mean_pull + cov_pull
            ).astype(jnp.bfloat16)
            return group_backward(pre_grad, weight).astype(jnp.bfloat16)

        def backward_bubble_step(operands):
            return jnp.zeros((micro_rows, channels), jnp.bfloat16)

        sent_back = lax.cond(
            in_range, backward_active_step, backward_bubble_step, (stored_item, incoming)
        )
        previous = lax.dynamic_index_in_dim(image_grads, slot_index, 0, keepdims=False)
        image_grads = lax.dynamic_update_index_in_dim(
            image_grads, jnp.where(in_range, sent_back, previous), slot_index, 0
        )
        incoming = from_behind(sent_back, "section", -1)
        return (incoming, image_grads)

    back_vars = (
        jnp.zeros((micro_rows, channels), jnp.bfloat16),
        jnp.zeros((MICRO, micro_rows, channels), jnp.bfloat16),
    )
    incoming, image_grads = lax.fori_loop(0, tick_count, backward_tick, back_vars)
    flat_grads = image_grads.reshape(group_rows, channels)
    own_term = jnp.where(
        position == 0,
        flat_grads.astype(jnp.float32),
        jnp.zeros((group_rows, channels), jnp.float32),
    )
    own_rows = lax.psum_scatter(
        own_term.astype(jnp.bfloat16), "section", scatter_dimension=0, tiled=True
    )
    return (own_rows[None], loss_value)


def solution(mesh):
    placed = (
        P("batch", None, None),
        P("section", None, None, None),
        P("section", None),
        P("section", None),
        P("section", None),
        P("section", None),
    )
    return jax.shard_map(
        shards,
        mesh=mesh,
        in_specs=placed,
        out_specs=(P("batch", "section", None), P()),
        check_vma=False,
    )
```

profile of v0, /device:TPU:8, one launch (start us, length us, event | category | flops | bytes accessed | tf_op | source)
XLA Modules:
  0.0 880.5 jit_solution(1067873683740494981)
XLA Ops:
  8.2 234.9 %while.37 = (s32[]{:T(128)}, bf16[32,1536]{1,0:T(8,128)(2,1)S(1)}, f32[8,32,1536]{2,1,0:T(8,128)S(1)}, f32[1536]{0:T(1024)S(1)}, s32[]{:T(128)}, /*index=5*/pred...) while((s32[]{:T(128)}, bf16[32,1536]{1,0:T(8,128)(2,1)S(1)}, ...), condition=%wide.region_4.5_spmd.clone, body=%wide.region_0.4_spmd.clone.sunk | while | flops 25708040 | bytes 3520875 | solution.py:96
  8.2 5.4 conditional.6
  17.3 5.4 conditional.6
  22.7 4.4 collective-permute-start.1
  29.3 5.4 conditional.6
  34.7 4.3 collective-permute-start.1
  41.2 5.4 conditional.6
  46.7 4.3 collective-permute-start.1
  53.2 5.4 conditional.6
  58.6 4.3 collective-permute-start.1
  65.1 5.4 conditional.6
  70.5 4.3 collective-permute-start.1
  77.1 5.4 conditional.6
  82.5 4.3 collective-permute-start.1
  89.0 5.4 conditional.6
  94.4 4.3 collective-permute-start.1
  101.6 9.0 %collective-permute-start.1 = (bf16[32,1536]{1,0:T(8,128)(2,1)S(1)}, bf16[32,1536]{1,0:T(8,128)(2,1)S(1)}, u32[]{:S(2)}, u32[]{:S(2)}) collective-permute-start(bf16[32,1536]{1,0:T(8,128)(2,1)S(1)} %get-tuple-element.842), channel_id=1, source_target_pairs={{0,32},{32,64},{64,96},{96,128},{128,160},{160,192},{192,224},{224... | collective-permute-start | bytes 294920 | tf_op jit(solution)/shard_map/while/body/eval_jaxpr/ppermute | solution.py:15
  113.6 4.3 collective-permute-start.1
  121.1 6.4 collective-permute-start.1
  130.4 5.5 collective-permute-start.1
  139.3 9.8 %collective-permute-start.1 = (bf16[32,1536]{1,0:T(8,128)(2,1)S(1)}, bf16[32,1536]{1,0:T(8,128)(2,1)S(1)}, u32[]{:S(2)}, u32[]{:S(2)}) collective-permute-start(bf16[32,1536]{1,0:T(8,128)(2,1)S(1)} %get-tuple-element.842), channel_id=1, source_target_pairs={{0,32},{32,64},{64,96},{96,128},{128,160},{160,192},{192,224},{224... | collective-permute-start | bytes 294920 | tf_op jit(solution)/shard_map/while/body/eval_jaxpr/ppermute | solution.py:15
  152.0 6.7 collective-permute-start.1
  161.6 9.6 %collective-permute-start.1 = (bf16[32,1536]{1,0:T(8,128)(2,1)S(1)}, bf16[32,1536]{1,0:T(8,128)(2,1)S(1)}, u32[]{:S(2)}, u32[]{:S(2)}) collective-permute-start(bf16[32,1536]{1,0:T(8,128)(2,1)S(1)} %get-tuple-element.842), channel_id=1, source_target_pairs={{0,32},{32,64},{64,96},{96,128},{128,160},{160,192},{192,224},{224... | collective-permute-start | bytes 294920 | tf_op jit(solution)/shard_map/while/body/eval_jaxpr/ppermute | solution.py:15
  175.0 5.5 collective-permute-start.1
  183.4 5.5 collective-permute-start.1
  191.8 5.5 collective-permute-start.1
  200.3 5.9 collective-permute-start.1
  209.1 5.6 collective-permute-start.1
  217.6 5.6 collective-permute-start.1
  226.1 5.5 collective-permute-start.1
  234.6 6.4 collective-permute-start.1
  243.1 64.5 %psum.21 = f32[1536]{0:T(1024)S(1)} all-reduce(f32[1536]{0:T(1024)S(1)} %get-tuple-element.603), channel_id=1, replica_groups=mesh['section'=16,'batch'=32] {'batch'}, use_global_device_ids=true, to_apply=%region_5.6 | all-reduce | flops 1536 | bytes 12288 | tf_op jit(solution)/shard_map/psum | solution.py:97
  313.2 5.1 fusion.9
  319.6 166.5 %all-reduce.2.cloned.1.call-done = f32[3,512,512]{2,1,0:T(8,128)} async-done(((f32[3,512,512]{2,1,0:T(8,128)}), f32[3,512,512]{2,1,0:T(8,128)}) %all-reduce.2.cloned.1.call-update) | async-done | bytes 3145744 | tf_op jit(solution)/shard_map/psum | solution.py:100
  486.1 3.8 multiply_reduce_fusion
  490.9 318.2 %while.36 = (s32[]{:T(128)}, bf16[32,1536]{1,0:T(8,128)(2,1)S(1)}, bf16[8,32,1536]{2,1,0:T(8,128)(2,1)}, s32[]{:T(128)}, f32[8,32,1536]{2,1,0:T(8,128)}, /*index...) while((s32[]{:T(128)}, bf16[32,1536]{1,0:T(8,128)(2,1)S(1)}, ...), condition=%wide.region_10.11_spmd, body=%wide.region_7.10_spmd.sunk | while | flops 328089600 | bytes 7834472 | solution.py:145
  520.2 4.7 collective-permute-done
  527.7 4.9 collective-permute-done
  535.5 6.1 collective-permute-done
  544.5 5.0 collective-permute-done
  552.3 4.8 collective-permute-done
  560.0 4.6 collective-permute-done
  567.5 4.9 collective-permute-done
  575.2 4.9 collective-permute-done
  582.9 4.9 collective-permute-done
  590.7 4.9 collective-permute-done
  598.4 89.0 %collective-permute-done = bf16[32,1536]{1,0:T(8,128)(2,1)S(1)} collective-permute-done((bf16[32,1536]{1,0:T(8,128)(2,1)S(1)}, bf16[32,1536]{1,0:T(8,128)(2,1)S(1)}, u32[]{:S(2)}, u32[]{:S(2)}) %collective-permute-start) | collective-permute-done | bytes 98336 | tf_op jit(solution)/shard_map/while/body/eval_jaxpr/ppermute | solution.py:15
  687.4 7.3 conditional.5
  697.6 5.6 collective-permute-done
  703.3 7.3 conditional.5
  713.4 5.7 collective-permute-done
  719.2 7.3 conditional.5
  729.4 4.6 collective-permute-done
  733.9 7.3 conditional.5
  744.1 4.7 collective-permute-done
  748.8 7.3 conditional.5
  759.0 5.3 collective-permute-done
  764.3 7.3 conditional.5
  774.4 4.9 collective-permute-done
  779.3 7.3 conditional.5
  789.5 5.8 collective-permute-done
  795.3 7.3 conditional.5
  812.5 27.6 %psum.23 = f32[]{:T(128)} all-reduce(f32[]{:T(128)S(6)} %add.132), channel_id=1, replica_groups=mesh['section'=16,'batch'=32] {'section'}, use_global_device_ids=true, to_apply=%region_14.15 | all-reduce | flops 1 | bytes 8 | tf_op jit(solution)/shard_map/psum | solution.py:104
  840.7 31.7 %reduce-scatter.2.cloned.1.call-done = bf16[16,1536]{1,0:T(8,128)(2,1)} async-done(((bf16[256,1536]{1,0:T(8,128)(2,1)}), bf16[16,1536]{1,0:T(8,128)(2,1)}) %reduce-scatter.2.cloned.1.call-update) | async-done | bytes 49168 | tf_op jit(solution)/shard_map/reduce_scatter | solution.py:152
  (425 shorter events, 270.5 us)
Async XLA Ops:
  7.2 479.0 %all-reduce.2.cloned.1.call-start = ((), (), s32[]{:S(2)}) async-start(), calls=%async_computation.1 | async-start | bytes 6291456 | tf_op jit(solution)/shard_map/psum | solution.py:100
  13.7 3.6 collective-permute-start.1
  22.7 6.6 collective-permute-start.1
  34.7 6.5 collective-permute-start.1
  46.7 6.5 collective-permute-start.1
  58.6 6.5 collective-permute-start.1
  70.5 6.5 collective-permute-start.1
  82.5 6.5 collective-permute-start.1
  94.4 6.5 collective-permute-start.1
  101.6 11.2 %collective-permute-start.1 = (bf16[32,1536]{1,0:T(8,128)(2,1)S(1)}, bf16[32,1536]{1,0:T(8,128)(2,1)S(1)}, u32[]{:S(2)}, u32[]{:S(2)}) collective-permute-start(bf16[32,1536]{1,0:T(8,128)(2,1)S(1)} %get-tuple-element.842), channel_id=1, source_target_pairs={{0,32},{32,64},{64,96},{96,128},{128,160},{160,192},{192,224},{224... | collective-permute-start | bytes 294920 | tf_op jit(solution)/shard_map/while/body/eval_jaxpr/ppermute | solution.py:15
  113.6 6.8 collective-permute-start.1
  121.1 8.6 collective-permute-start.1
  130.4 8.2 collective-permute-start.1
  139.3 12.0 %collective-permute-start.1 = (bf16[32,1536]{1,0:T(8,128)(2,1)S(1)}, bf16[32,1536]{1,0:T(8,128)(2,1)S(1)}, u32[]{:S(2)}, u32[]{:S(2)}) collective-permute-start(bf16[32,1536]{1,0:T(8,128)(2,1)S(1)} %get-tuple-element.842), channel_id=1, source_target_pairs={{0,32},{32,64},{64,96},{96,128},{128,160},{160,192},{192,224},{224... | collective-permute-start | bytes 294920 | tf_op jit(solution)/shard_map/while/body/eval_jaxpr/ppermute | solution.py:15
  152.0 8.9 %collective-permute-start.1 = (bf16[32,1536]{1,0:T(8,128)(2,1)S(1)}, bf16[32,1536]{1,0:T(8,128)(2,1)S(1)}, u32[]{:S(2)}, u32[]{:S(2)}) collective-permute-start(bf16[32,1536]{1,0:T(8,128)(2,1)S(1)} %get-tuple-element.842), channel_id=1, source_target_pairs={{0,32},{32,64},{64,96},{96,128},{128,160},{160,192},{192,224},{224... | collective-permute-start | bytes 294920 | tf_op jit(solution)/shard_map/while/body/eval_jaxpr/ppermute | solution.py:15
  161.6 12.6 %collective-permute-start.1 = (bf16[32,1536]{1,0:T(8,128)(2,1)S(1)}, bf16[32,1536]{1,0:T(8,128)(2,1)S(1)}, u32[]{:S(2)}, u32[]{:S(2)}) collective-permute-start(bf16[32,1536]{1,0:T(8,128)(2,1)S(1)} %get-tuple-element.842), channel_id=1, source_target_pairs={{0,32},{32,64},{64,96},{96,128},{128,160},{160,192},{192,224},{224... | collective-permute-start | bytes 294920 | tf_op jit(solution)/shard_map/while/body/eval_jaxpr/ppermute | solution.py:15
  175.0 7.7 collective-permute-start.1
  183.4 7.7 collective-permute-start.1
  191.8 7.7 collective-permute-start.1
  200.3 8.1 collective-permute-start.1
  209.1 7.8 collective-permute-start.1
  217.6 7.8 collective-permute-start.1
  226.1 7.7 collective-permute-start.1
  234.6 8.6 collective-permute-start.1
  243.1 70.1 %copy-start = (f32[8,32,1536]{2,1,0:T(8,128)}, f32[8,32,1536]{2,1,0:T(8,128)S(1)}, u32[]{:S(2)}) copy-start(f32[8,32,1536]{2,1,0:T(8,128)S(1)} %get-tuple-element.900) | copy-start | bytes 4718596
  318.4 554.1 %reduce-scatter.2.cloned.1.call-start = ((), (), s32[]{:S(2)}) async-start(), calls=%async_computation.2 | async-start | bytes 835584 | tf_op jit(solution)/shard_map/reduce_scatter | solution.py:152
  319.6 171.3 %copy-start.1 = (f32[1,1536]{1,0:T(1,128)S(1)}, f32[1,1536]{1,0:T(1,128)}, u32[]{:S(2)}) copy-start(f32[1,1536]{1,0:T(1,128)} %get-tuple-element.958) | copy-start | bytes 18436
  319.6 171.3 %copy-start.2 = (f32[1,1536]{1,0:T(1,128)S(1)}, f32[1,1536]{1,0:T(1,128)}, u32[]{:S(2)}) copy-start(f32[1,1536]{1,0:T(1,128)} %get-tuple-element.959) | copy-start | bytes 18436
  491.0 6.7 collective-permute-start
  497.7 6.5 collective-permute-start
  504.2 6.5 collective-permute-start
  510.8 6.5 collective-permute-start
  517.3 7.6 collective-permute-start
  524.9 7.7 collective-permute-start
  532.6 9.0 %collective-permute-start = (bf16[32,1536]{1,0:T(8,128)(2,1)S(1)}, bf16[32,1536]{1,0:T(8,128)(2,1)S(1)}, u32[]{:S(2)}, u32[]{:S(2)}) collective-permute-start(bf16[32,1536]{1,0:T(8,128)(2,1)S(1)} %get-tuple-element.944), channel_id=1, source_target_pairs={{32,0},{64,32},{96,64},{128,96},{160,128},{192,160},{224,192},{256... | collective-permute-start | bytes 294920 | tf_op jit(solution)/shard_map/while/body/eval_jaxpr/ppermute | solution.py:15
  541.6 7.9 collective-permute-start
  549.5 7.6 collective-permute-start
  557.1 7.4 collective-permute-start
  564.6 7.7 collective-permute-start
  572.3 7.7 collective-permute-start
  580.1 7.7 collective-permute-start
  587.8 7.7 collective-permute-start
  595.6 91.9 %collective-permute-start = (bf16[32,1536]{1,0:T(8,128)(2,1)S(1)}, bf16[32,1536]{1,0:T(8,128)(2,1)S(1)}, u32[]{:S(2)}, u32[]{:S(2)}) collective-permute-start(bf16[32,1536]{1,0:T(8,128)(2,1)S(1)} %get-tuple-element.944), channel_id=1, source_target_pairs={{32,0},{64,32},{96,64},{128,96},{160,128},{192,160},{224,192},{256... | collective-permute-start | bytes 294920 | tf_op jit(solution)/shard_map/while/body/eval_jaxpr/ppermute | solution.py:15
  694.7 8.5 collective-permute-start
  710.6 8.6 collective-permute-start
  726.5 7.5 collective-permute-start
  741.2 7.5 collective-permute-start
  756.1 8.2 collective-permute-start
  771.6 7.7 collective-permute-start
  786.6 8.7 collective-permute-start
  802.6 6.6 collective-permute-start
Sparse Core Ops, SparseCore 0:
  318.5 167.5 all-reduce.1
  811.4 61.0 reduce-scatter.1
where the time goes:
time: 885 us; the launch traced here: 880 us
  waiting for transfers between devices  434 us (49%)
  starting transfers between devices  158 us (18%)
  blocking collectives  92.1 us (10%)
  other arithmetic  70.8 us (8%)
  local copies, waits for them, and re-layouts  62.6 us (7%)
  matrix products  43.3 us (5%)
  between operations  17.1 us (2%)
    ppermute x46, waiting for transfers between devices, from_behind(): lax.ppermute(value, axis, [(source, source + steps) for source in range(f...  236 us
    psum x1, waiting for transfers between devices, shards(): lax.psum(block_gram(flat_saved, batch_mean, BLOCK), 'batch') / row_total  166 us
    ppermute x46, starting transfers between devices, from_behind(): lax.ppermute(value, axis, [(source, source + steps) for source in range(f...  158 us
    psum x1, blocking collectives, shards(): total_sum = lax.psum(sum_pre, 'batch')  64.5 us
    reduce_scatter x1, waiting for transfers between devices, shards(): lax.psum_scatter(own_term.astype(jnp.bfloat16), 'section', scatter_dimens...  31.7 us
    psum x1, blocking collectives, shards(): loss_value = lax.psum(layer_term, 'section') / (sections * channels)  27.6 us
    dynamic_slice x23, local copies, waits for them, and re-layouts, backward_tick(): lax.dynamic_index_in_dim(image_grads, slot_index, 0, keepdims=False)  20.8 us
  transfers between devices with their start and end apart: 48, of which 48 were waited for; matrix products, arithmetic and copies ran while one was open for 5% of the time, Pallas kernels for 0%

commit v1 on v0

--- a/solution.py
+++ b/solution.py
@@ -94,7 +94,7 @@
         jnp.zeros(gram_shape, jnp.float32),
     )
     incoming, stored, sum_pre, sum_gram = lax.fori_loop(0, tick_count, forward_tick, start_vars)
-    total_sum = lax.psum(sum_pre, "batch")
+    total_sum = jnp.sum(lax.all_gather(sum_pre, "batch"), axis=0)
     batch_mean = total_sum / row_total
     flat_saved = stored.reshape(group_rows, channels)
     covariance = lax.psum(block_gram(flat_saved, batch_mean, BLOCK), "batch") / row_total

time: 885 us -> 847 us (0.957)
  blocking collectives: 92.1 us -> 55.8 us
    psum x1 -> x0, blocking collectives: 64.5 us -> none  [shards(): total_sum = lax.psum(sum_pre, 'batch')]
    all_gather x0 -> x1, blocking collectives: none -> 28.2 us  [shards(): total_sum = jnp.sum(lax.all_gather(sum_pre, 'batch'), axis=0)]
  transfers between devices with their start and end apart: 48 -> 48, of which waited for: 48 -> 48; matrix products, arithmetic and copies ran while one was open for 5% -> 6% of each run, Pallas kernels for 0% -> 0%
where the time goes in v1:
time: 847 us; the launch traced here: 842 us
  waiting for transfers between devices  432 us (51%)
  starting transfers between devices  158 us (19%)
  other arithmetic  70.9 us (8%)
  local copies, waits for them, and re-layouts  62.6 us (7%)
  blocking collectives  55.8 us (7%)
  matrix products  43.3 us (5%)
  between operations  17.1 us (2%)
    ppermute x46, waiting for transfers between devices, from_behind(): lax.ppermute(value, axis, [(source, source + steps) for source in range(f...  236 us
    psum x1, waiting for transfers between devices, shards(): lax.psum(block_gram(flat_saved, batch_mean, BLOCK), 'batch') / row_total  164 us
    ppermute x46, starting transfers between devices, from_behind(): lax.ppermute(value, axis, [(source, source + steps) for source in range(f...  158 us
    reduce_scatter x1, waiting for transfers between devices, shards(): lax.psum_scatter(own_term.astype(jnp.bfloat16), 'section', scatter_dimens...  31.7 us
    all_gather x1, blocking collectives, shards(): total_sum = jnp.sum(lax.all_gather(sum_pre, 'batch'), axis=0)  28.2 us
    psum x1, blocking collectives, shards(): loss_value = lax.psum(layer_term, 'section') / (sections * channels)  27.6 us
    dynamic_slice x23, local copies, waits for them, and re-layouts, backward_tick(): lax.dynamic_index_in_dim(image_grads, slot_index, 0, keepdims=False)  20.8 us
  transfers between devices with their start and end apart: 48, of which 48 were waited for; matrix products, arithmetic and copies ran while one was open for 6% of the time, Pallas kernels for 0%

profile of v1, /device:TPU:8, one launch (start us, length us, event | category | flops | bytes accessed | tf_op | source)
XLA Modules:
  0.0 842.2 jit_solution(1508336327803027534)
XLA Ops:
  8.2 234.9 %while.37 = (s32[]{:T(128)}, bf16[32,1536]{1,0:T(8,128)(2,1)S(1)}, f32[8,32,1536]{2,1,0:T(8,128)S(1)}, f32[1536]{0:T(1024)S(1)}, s32[]{:T(128)}, /*index=5*/pred...) while((s32[]{:T(128)}, bf16[32,1536]{1,0:T(8,128)(2,1)S(1)}, ...), condition=%wide.region_4.5_spmd.clone, body=%wide.region_0.4_spmd.clone.sunk | while | flops 25708040 | bytes 3520875 | solution.py:96
  8.2 5.4 conditional.6
  17.3 5.4 conditional.6
  22.7 4.4 collective-permute-start.1
  29.3 5.4 conditional.6
  34.7 4.3 collective-permute-start.1
  41.2 5.4 conditional.6
  46.7 4.3 collective-permute-start.1
  53.2 5.4 conditional.6
  58.6 4.3 collective-permute-start.1
  65.1 5.4 conditional.6
  70.5 4.3 collective-permute-start.1
  77.1 5.4 conditional.6
  82.5 4.3 collective-permute-start.1
  89.0 5.4 conditional.6
  94.4 4.3 collective-permute-start.1
  101.6 9.0 %collective-permute-start.1 = (bf16[32,1536]{1,0:T(8,128)(2,1)S(1)}, bf16[32,1536]{1,0:T(8,128)(2,1)S(1)}, u32[]{:S(2)}, u32[]{:S(2)}) collective-permute-start(bf16[32,1536]{1,0:T(8,128)(2,1)S(1)} %get-tuple-element.842), channel_id=1, source_target_pairs={{0,32},{32,64},{64,96},{96,128},{128,160},{160,192},{192,224},{224... | collective-permute-start | bytes 294920 | tf_op jit(solution)/shard_map/while/body/eval_jaxpr/ppermute | solution.py:15
  113.6 4.3 collective-permute-start.1
  121.1 6.4 collective-permute-start.1
  130.4 5.5 collective-permute-start.1
  139.3 9.8 %collective-permute-start.1 = (bf16[32,1536]{1,0:T(8,128)(2,1)S(1)}, bf16[32,1536]{1,0:T(8,128)(2,1)S(1)}, u32[]{:S(2)}, u32[]{:S(2)}) collective-permute-start(bf16[32,1536]{1,0:T(8,128)(2,1)S(1)} %get-tuple-element.842), channel_id=1, source_target_pairs={{0,32},{32,64},{64,96},{96,128},{128,160},{160,192},{192,224},{224... | collective-permute-start | bytes 294920 | tf_op jit(solution)/shard_map/while/body/eval_jaxpr/ppermute | solution.py:15
  152.0 6.7 collective-permute-start.1
  161.6 9.6 %collective-permute-start.1 = (bf16[32,1536]{1,0:T(8,128)(2,1)S(1)}, bf16[32,1536]{1,0:T(8,128)(2,1)S(1)}, u32[]{:S(2)}, u32[]{:S(2)}) collective-permute-start(bf16[32,1536]{1,0:T(8,128)(2,1)S(1)} %get-tuple-element.842), channel_id=1, source_target_pairs={{0,32},{32,64},{64,96},{96,128},{128,160},{160,192},{192,224},{224... | collective-permute-start | bytes 294920 | tf_op jit(solution)/shard_map/while/body/eval_jaxpr/ppermute | solution.py:15
  175.0 5.5 collective-permute-start.1
  183.4 5.5 collective-permute-start.1
  191.8 5.5 collective-permute-start.1
  200.3 5.9 collective-permute-start.1
  209.1 5.6 collective-permute-start.1
  217.6 5.6 collective-permute-start.1
  226.1 5.5 collective-permute-start.1
  234.6 6.4 collective-permute-start.1
  243.1 28.2 %all-gather.1 = f32[32,1,1536]{2,1,0:T(1,128)S(1)} all-gather(f32[1,1,1536]{2,1,0:T(1,128)S(1)} %reshape.74), channel_id=2, replica_groups=mesh['section'=16,'batch'=32] {'batch'}, dimensions={0}, use_global_device_ids=true | all-gather | bytes 202752 | tf_op jit(solution)/shard_map/all_gather | solution.py:97
  277.0 5.1 fusion.9
  283.4 164.5 %all-reduce.2.cloned.1.call-done = f32[3,512,512]{2,1,0:T(8,128)} async-done(((f32[3,512,512]{2,1,0:T(8,128)}), f32[3,512,512]{2,1,0:T(8,128)}) %all-reduce.2.cloned.1.call-update) | async-done | bytes 3145744 | tf_op jit(solution)/shard_map/psum | solution.py:100
  447.9 3.8 multiply_reduce_fusion
  452.7 318.2 %while.36 = (s32[]{:T(128)}, bf16[32,1536]{1,0:T(8,128)(2,1)S(1)}, bf16[8,32,1536]{2,1,0:T(8,128)(2,1)}, s32[]{:T(128)}, f32[8,32,1536]{2,1,0:T(8,128)}, /*index...) while((s32[]{:T(128)}, bf16[32,1536]{1,0:T(8,128)(2,1)S(1)}, ...), condition=%wide.region_10.11_spmd, body=%wide.region_7.10_spmd.sunk | while | flops 328089600 | bytes 7834472 | solution.py:145
  481.9 4.7 collective-permute-done
  489.5 4.9 collective-permute-done
  497.2 6.1 collective-permute-done
  506.2 5.0 collective-permute-done
  514.1 4.8 collective-permute-done
  521.7 4.6 collective-permute-done
  529.2 4.9 collective-permute-done
  537.0 4.9 collective-permute-done
  544.7 4.9 collective-permute-done
  552.4 4.9 collective-permute-done
  560.2 89.0 %collective-permute-done = bf16[32,1536]{1,0:T(8,128)(2,1)S(1)} collective-permute-done((bf16[32,1536]{1,0:T(8,128)(2,1)S(1)}, bf16[32,1536]{1,0:T(8,128)(2,1)S(1)}, u32[]{:S(2)}, u32[]{:S(2)}) %collective-permute-start) | collective-permute-done | bytes 98336 | tf_op jit(solution)/shard_map/while/body/eval_jaxpr/ppermute | solution.py:15
  649.2 7.3 conditional.5
  659.4 5.6 collective-permute-done
  665.0 7.3 conditional.5
  675.2 5.7 collective-permute-done
  680.9 7.3 conditional.5
  691.1 4.6 collective-permute-done
  695.7 7.3 conditional.5
  705.9 4.7 collective-permute-done
  710.5 7.3 conditional.5
  720.7 5.3 collective-permute-done
  726.0 7.3 conditional.5
  736.2 4.9 collective-permute-done
  741.1 7.3 conditional.5
  751.2 5.8 collective-permute-done
  757.0 7.3 conditional.5
  774.2 27.6 %psum.15 = f32[]{:T(128)} all-reduce(f32[]{:T(128)S(6)} %add.130), channel_id=1, replica_groups=mesh['section'=16,'batch'=32] {'section'}, use_global_device_ids=true, to_apply=%region_14.15 | all-reduce | flops 1 | bytes 8 | tf_op jit(solution)/shard_map/psum | solution.py:104
  802.5 31.7 %reduce-scatter.2.cloned.1.call-done = bf16[16,1536]{1,0:T(8,128)(2,1)} async-done(((bf16[256,1536]{1,0:T(8,128)(2,1)}), bf16[16,1536]{1,0:T(8,128)(2,1)}) %reduce-scatter.2.cloned.1.call-update) | async-done | bytes 49168 | tf_op jit(solution)/shard_map/reduce_scatter | solution.py:152
  (427 shorter events, 270.7 us)
Async XLA Ops:
  7.2 440.7 %all-reduce.2.cloned.1.call-start = ((), (), s32[]{:S(2)}) async-start(), calls=%async_computation.1 | async-start | bytes 6291456 | tf_op jit(solution)/shard_map/psum | solution.py:100
  13.7 3.6 collective-permute-start.1
  22.7 6.6 collective-permute-start.1
  34.7 6.5 collective-permute-start.1
  46.7 6.5 collective-permute-start.1
  58.6 6.5 collective-permute-start.1
  70.5 6.5 collective-permute-start.1
  82.5 6.5 collective-permute-start.1
  94.4 6.5 collective-permute-start.1
  101.6 11.2 %collective-permute-start.1 = (bf16[32,1536]{1,0:T(8,128)(2,1)S(1)}, bf16[32,1536]{1,0:T(8,128)(2,1)S(1)}, u32[]{:S(2)}, u32[]{:S(2)}) collective-permute-start(bf16[32,1536]{1,0:T(8,128)(2,1)S(1)} %get-tuple-element.842), channel_id=1, source_target_pairs={{0,32},{32,64},{64,96},{96,128},{128,160},{160,192},{192,224},{224... | collective-permute-start | bytes 294920 | tf_op jit(solution)/shard_map/while/body/eval_jaxpr/ppermute | solution.py:15
  113.6 6.8 collective-permute-start.1
  121.1 8.6 %collective-permute-start.1 = (bf16[32,1536]{1,0:T(8,128)(2,1)S(1)}, bf16[32,1536]{1,0:T(8,128)(2,1)S(1)}, u32[]{:S(2)}, u32[]{:S(2)}) collective-permute-start(bf16[32,1536]{1,0:T(8,128)(2,1)S(1)} %get-tuple-element.842), channel_id=1, source_target_pairs={{0,32},{32,64},{64,96},{96,128},{128,160},{160,192},{192,224},{224... | collective-permute-start | bytes 294920 | tf_op jit(solution)/shard_map/while/body/eval_jaxpr/ppermute | solution.py:15
  130.4 8.2 collective-permute-start.1
  139.3 12.0 %collective-permute-start.1 = (bf16[32,1536]{1,0:T(8,128)(2,1)S(1)}, bf16[32,1536]{1,0:T(8,128)(2,1)S(1)}, u32[]{:S(2)}, u32[]{:S(2)}) collective-permute-start(bf16[32,1536]{1,0:T(8,128)(2,1)S(1)} %get-tuple-element.842), channel_id=1, source_target_pairs={{0,32},{32,64},{64,96},{96,128},{128,160},{160,192},{192,224},{224... | collective-permute-start | bytes 294920 | tf_op jit(solution)/shard_map/while/body/eval_jaxpr/ppermute | solution.py:15
  152.0 8.9 %collective-permute-start.1 = (bf16[32,1536]{1,0:T(8,128)(2,1)S(1)}, bf16[32,1536]{1,0:T(8,128)(2,1)S(1)}, u32[]{:S(2)}, u32[]{:S(2)}) collective-permute-start(bf16[32,1536]{1,0:T(8,128)(2,1)S(1)} %get-tuple-element.842), channel_id=1, source_target_pairs={{0,32},{32,64},{64,96},{96,128},{128,160},{160,192},{192,224},{224... | collective-permute-start | bytes 294920 | tf_op jit(solution)/shard_map/while/body/eval_jaxpr/ppermute | solution.py:15
  161.6 12.6 %collective-permute-start.1 = (bf16[32,1536]{1,0:T(8,128)(2,1)S(1)}, bf16[32,1536]{1,0:T(8,128)(2,1)S(1)}, u32[]{:S(2)}, u32[]{:S(2)}) collective-permute-start(bf16[32,1536]{1,0:T(8,128)(2,1)S(1)} %get-tuple-element.842), channel_id=1, source_target_pairs={{0,32},{32,64},{64,96},{96,128},{128,160},{160,192},{192,224},{224... | collective-permute-start | bytes 294920 | tf_op jit(solution)/shard_map/while/body/eval_jaxpr/ppermute | solution.py:15
  175.0 7.7 collective-permute-start.1
  183.4 7.7 collective-permute-start.1
  191.8 7.7 collective-permute-start.1
  200.3 8.1 collective-permute-start.1
  209.1 7.8 collective-permute-start.1
  217.6 7.8 collective-permute-start.1
  226.1 7.7 collective-permute-start.1
  234.6 8.6 %collective-permute-start.1 = (bf16[32,1536]{1,0:T(8,128)(2,1)S(1)}, bf16[32,1536]{1,0:T(8,128)(2,1)S(1)}, u32[]{:S(2)}, u32[]{:S(2)}) collective-permute-start(bf16[32,1536]{1,0:T(8,128)(2,1)S(1)} %get-tuple-element.842), channel_id=1, source_target_pairs={{0,32},{32,64},{64,96},{96,128},{128,160},{160,192},{192,224},{224... | collective-permute-start | bytes 294920 | tf_op jit(solution)/shard_map/while/body/eval_jaxpr/ppermute | solution.py:15
  243.1 33.9 %copy-start = (f32[8,32,1536]{2,1,0:T(8,128)}, f32[8,32,1536]{2,1,0:T(8,128)S(1)}, u32[]{:S(2)}) copy-start(f32[8,32,1536]{2,1,0:T(8,128)S(1)} %get-tuple-element.900) | copy-start | bytes 4718596
  282.2 552.1 %reduce-scatter.2.cloned.1.call-start = ((), (), s32[]{:S(2)}) async-start(), calls=%async_computation.2 | async-start | bytes 835584 | tf_op jit(solution)/shard_map/reduce_scatter | solution.py:152
  283.4 169.3 %copy-start.1 = (f32[1,1536]{1,0:T(1,128)S(1)}, f32[1,1536]{1,0:T(1,128)}, u32[]{:S(2)}) copy-start(f32[1,1536]{1,0:T(1,128)} %get-tuple-element.958) | copy-start | bytes 18436
  283.4 169.3 %copy-start.2 = (f32[1,1536]{1,0:T(1,128)S(1)}, f32[1,1536]{1,0:T(1,128)}, u32[]{:S(2)}) copy-start(f32[1,1536]{1,0:T(1,128)} %get-tuple-element.959) | copy-start | bytes 18436
  452.8 6.7 collective-permute-start
  459.5 6.5 collective-permute-start
  466.0 6.5 collective-permute-start
  472.5 6.5 collective-permute-start
  479.1 7.6 collective-permute-start
  486.6 7.7 collective-permute-start
  494.4 9.0 %collective-permute-start = (bf16[32,1536]{1,0:T(8,128)(2,1)S(1)}, bf16[32,1536]{1,0:T(8,128)(2,1)S(1)}, u32[]{:S(2)}, u32[]{:S(2)}) collective-permute-start(bf16[32,1536]{1,0:T(8,128)(2,1)S(1)} %get-tuple-element.944), channel_id=1, source_target_pairs={{32,0},{64,32},{96,64},{128,96},{160,128},{192,160},{224,192},{256... | collective-permute-start | bytes 294920 | tf_op jit(solution)/shard_map/while/body/eval_jaxpr/ppermute | solution.py:15
  503.4 7.9 collective-permute-start
  511.2 7.6 collective-permute-start
  518.9 7.4 collective-permute-start
  526.3 7.7 collective-permute-start
  534.1 7.7 collective-permute-start
  541.8 7.7 collective-permute-start
  549.6 7.7 collective-permute-start
  557.3 91.9 %collective-permute-start = (bf16[32,1536]{1,0:T(8,128)(2,1)S(1)}, bf16[32,1536]{1,0:T(8,128)(2,1)S(1)}, u32[]{:S(2)}, u32[]{:S(2)}) collective-permute-start(bf16[32,1536]{1,0:T(8,128)(2,1)S(1)} %get-tuple-element.944), channel_id=1, source_target_pairs={{32,0},{64,32},{96,64},{128,96},{160,128},{192,160},{224,192},{256... | collective-permute-start | bytes 294920 | tf_op jit(solution)/shard_map/while/body/eval_jaxpr/ppermute | solution.py:15
  656.5 8.5 %collective-permute-start = (bf16[32,1536]{1,0:T(8,128)(2,1)S(1)}, bf16[32,1536]{1,0:T(8,128)(2,1)S(1)}, u32[]{:S(2)}, u32[]{:S(2)}) collective-permute-start(bf16[32,1536]{1,0:T(8,128)(2,1)S(1)} %get-tuple-element.944), channel_id=1, source_target_pairs={{32,0},{64,32},{96,64},{128,96},{160,128},{192,160},{224,192},{256... | collective-permute-start | bytes 294920 | tf_op jit(solution)/shard_map/while/body/eval_jaxpr/ppermute | solution.py:15
  672.3 8.6 %collective-permute-start = (bf16[32,1536]{1,0:T(8,128)(2,1)S(1)}, bf16[32,1536]{1,0:T(8,128)(2,1)S(1)}, u32[]{:S(2)}, u32[]{:S(2)}) collective-permute-start(bf16[32,1536]{1,0:T(8,128)(2,1)S(1)} %get-tuple-element.944), channel_id=1, source_target_pairs={{32,0},{64,32},{96,64},{128,96},{160,128},{192,160},{224,192},{256... | collective-permute-start | bytes 294920 | tf_op jit(solution)/shard_map/while/body/eval_jaxpr/ppermute | solution.py:15
  688.2 7.5 collective-permute-start
  703.0 7.5 collective-permute-start
  717.9 8.2 collective-permute-start
  733.3 7.7 collective-permute-start
  748.4 8.7 %collective-permute-start = (bf16[32,1536]{1,0:T(8,128)(2,1)S(1)}, bf16[32,1536]{1,0:T(8,128)(2,1)S(1)}, u32[]{:S(2)}, u32[]{:S(2)}) collective-permute-start(bf16[32,1536]{1,0:T(8,128)(2,1)S(1)} %get-tuple-element.944), channel_id=1, source_target_pairs={{32,0},{64,32},{96,64},{128,96},{160,128},{192,160},{224,192},{256... | collective-permute-start | bytes 294920 | tf_op jit(solution)/shard_map/while/body/eval_jaxpr/ppermute | solution.py:15
  764.3 6.6 collective-permute-start
Sparse Core Ops, SparseCore 0:
  282.3 165.5 all-reduce.1
  773.2 61.0 reduce-scatter.1
